TPU v7x, 32 devices: a whole 2x2x4 slice. The times are simulated.
32 devices in a mesh: tm: 8 (over z, x), clip: 4 (over y, core).
Axes of the slice: x: 2, y: 2, z: 4, core: 2. Of those that a mesh axis runs over, the one named last changes fastest.
Arguments:
- video: float32 [4, 8, 16, 32, 320], P('clip', 'tm'), may hold values from -6 to 6
- spatial_w: bfloat16 [9, 320, 320], P(None, 'clip'), may hold values from -0.109375 to 0.109375
- spatial_b: float32 [320], replicated, may hold values from -3 to 3
- temporal_w: float32 [3, 320, 320], P(None, 'clip'), may hold values from -0.1875 to 0.1875
- cotangent: float32 [4, 8, 16, 32, 320], P('clip', 'tm'), may hold values from -6 to 6
Outputs:
- output: float32 [4, 8, 16, 32, 320], P('clip', 'tm')
- grad_video: float32 [4, 8, 16, 32, 320], P('clip', 'tm')
- grad_temporal: float32 [3, 320, 320], P(None, 'clip')
All inputs are finite; a program needn't handle non-finite values.
Results may differ from a plain program's by a relative error of at most 0.0049.
Values may be sent and summed in bfloat16 or wider, within the bound.
A program may use at most 64 MiB of HBM per device.

v0:
```python
import math
import jax
import jax.numpy as jnp
from jax import lax
from jax.sharding import PartitionSpec as P


def padded_2(cells, sides, width):
    for axis, dim in sides:
        count = lax.axis_size(axis)
        ends = count - 1
        head = lax.slice_in_dim(cells, 0, width, axis=dim)
        tail = lax.slice_in_dim(cells, cells.shape[dim] - width, cells.shape[dim], axis=dim)
        cells = jnp.concatenate(
            [
                lax.ppermute(tail, axis, [(i, (i + 1) % count) for i in range(ends)]),
                cells,
                lax.ppermute(head, axis, [((i + 1) % count, i) for i in range(ends)]),
            ],
            axis=dim,
        )
    return cells


def outer_dot(left, right):
    return lax.dot_general(
        left, right, (((0,), (0,)), ((), ())), preferred_element_type=jnp.float32
    )


def transpose_dot(left, right):
    return lax.dot_general(
        left, right, (((1,), (1,)), ((), ())), preferred_element_type=jnp.float32
    )


def on_device(video, spatial_w, spatial_b, temporal_w, cotangent):
    clips, frames, height, width, chans = video.shape
    row_count = clips * frames * height * width
    video_b = video.astype(jnp.bfloat16)
    padded = jnp.pad(video_b, ((0, 0), (0, 0), (1, 1), (1, 1), (0, 0)))
    temporal_b = temporal_w.astype(jnp.bfloat16)
    spatial_all, temporal_all = (
        lax.all_gather(spatial_w, "clip", axis=1, tiled=True),
        lax.all_gather(temporal_b, "clip", axis=1, tiled=True),
    )
    spatial = jnp.zeros((row_count, chans), jnp.float32)
    for shift_y in range(3):
        for shift_x in range(3):
            window = padded[:, :, shift_y : shift_y + height, shift_x : shift_x + width, :].reshape(
                row_count, chans
            )
            spatial = spatial + jnp.dot(
                window, spatial_all[3 * shift_y + shift_x], preferred_element_type=jnp.float32
            )
    spatial = spatial + spatial_b
    sigmoid_s = jax.nn.sigmoid(spatial)
    hidden = (spatial * sigmoid_s).astype(jnp.bfloat16).reshape(clips, frames, height, width, chans)
    hidden_pad = padded_2(hidden, (("tm", 1),), 1)
    temporal = jnp.zeros((row_count, chans), jnp.float32)
    for kernel_tap in range(3):
        shifted = hidden_pad[:, kernel_tap : kernel_tap + frames].reshape(row_count, chans)
        temporal = temporal + jnp.dot(
            shifted, temporal_all[kernel_tap], preferred_element_type=jnp.float32
        )
    output = video + temporal.reshape(video.shape)
    cot_b = cotangent.astype(jnp.bfloat16)
    cot_flat = cot_b.reshape(row_count, chans)
    cot_pad = padded_2(cot_b, (("tm", 1),), 1)
    grad_hidden = jnp.zeros((row_count, chans), jnp.float32)
    grads = []
    for kernel_tap in range(3):
        shifted_cot = cot_pad[:, 2 - kernel_tap : 2 - kernel_tap + frames].reshape(row_count, chans)
        grad_hidden = grad_hidden + transpose_dot(shifted_cot, temporal_all[kernel_tap])
        shifted_hid = hidden_pad[:, kernel_tap : kernel_tap + frames].reshape(row_count, chans)
        grads.append(outer_dot(shifted_hid, cot_flat))
    local_grad = jnp.stack(grads)
    total_rows = row_count * lax.axis_size("tm") * lax.axis_size("clip")
    summed = lax.psum(local_grad, "tm")
    owned = lax.psum_scatter(summed, "clip", scatter_dimension=1, tiled=True)
    grad_temporal = owned * (1.0 / math.sqrt(total_rows))
    grad_spatial = (grad_hidden * sigmoid_s * (1.0 + spatial * (1.0 - sigmoid_s))).astype(
        jnp.bfloat16
    )
    grad_frames = jnp.pad(
        grad_spatial.reshape(clips, frames, height, width, chans),
        ((0, 0), (0, 0), (1, 1), (1, 1), (0, 0)),
    )
    grad_acc = cotangent.reshape(row_count, chans)
    for shift_y in range(3):
        for shift_x in range(3):
            window = grad_frames[
                :, :, 2 - shift_y : 2 - shift_y + height, 2 - shift_x : 2 - shift_x + width, :
            ].reshape(row_count, chans)
            grad_acc = grad_acc + transpose_dot(window, spatial_all[3 * shift_y + shift_x])
    grad_video = grad_acc.reshape(video.shape)
    return (output, grad_video, grad_temporal)


def solution(mesh):
    return jax.shard_map(
        on_device,
        mesh=mesh,
        in_specs=(
            P("clip", "tm", None, None, None),
            P(None, "clip", None),
            P(),
            P(None, "clip", None),
            P("clip", "tm", None, None, None),
        ),
        out_specs=(
            P("clip", "tm", None, None, None),
            P("clip", "tm", None, None, None),
            P(None, "clip", None),
        ),
        check_vma=False,
    )
```

profile of v0, /device:TPU:0, one launch (start us, length us, event | category | flops | bytes accessed | tf_op | source)
XLA Modules:
  0.0 184.8 jit_solution(11059689400053077663)
XLA Ops:
  7.2 0.0 copy-start.4
  7.2 0.0 all-gather.2.cloned.1.call-start
  7.2 0.7 all-gather.2.cloned.1.call-update
  7.9 0.0 reduce-scatter.2.cloned.1.call-start
  8.0 1.2 convert_element_type.21
  9.2 4.9 %collective-permute-start.3 = (bf16[1,1,16,32,320]{4,3,2,1,0:T(8,128)(2,1)S(1)}, bf16[1,1,16,32,320]{4,3,2,1,0:T(8,128)(2,1)S(1)}, u32[]{:S(2)}, u32[]{:S(2)}) collective-permute-start(bf16[1,1,16,32,320]{4,3,2,1,0:T(8,128)(2,1)S(1)} %convert_element_type.21), channel_id=1, source_target_pairs={{0,4},{4,8},{8,12},{12,16},{16,20},{20,24},{24,28},{1,5},{5,9},{9,... | collective-permute-start | bytes 983048 | tf_op jit(solution)/shard_map/ppermute | solution.py:16
  14.1 1.3 collective-permute-start.2
  15.5 0.0 copy-start.3
  15.5 10.1 %all_gather.7 = bf16[3,320,320]{2,1,0:T(8,128)(2,1)S(1)} all-gather(bf16[3,80,320]{2,1,0:T(8,128)(2,1)S(1)} %convert_element_type.20), channel_id=1, replica_groups=mesh['tm'=8,'clip'=4] {'clip'}, dimensions={1}, use_global_device_ids=true | all-gather | bytes 768000 | tf_op jit(solution)/shard_map/all_gather | solution.py:45
  25.6 1.8 pad_slice_fusion.8
  27.4 1.1 copy.16
  28.5 1.2 fusion.19
  29.7 1.1 collective-permute-done.3
  30.8 1.2 fusion.21
  32.0 4.5 %all-gather.2.cloned.1.call-done = bf16[9,320,320]{2,1,0:T(8,128)(2,1)} async-done(((bf16[9,80,320]{2,1,0:T(8,128)(2,1)}), bf16[9,320,320]{2,1,0:T(8,128)(2,1)}) %all-gather.2.cloned.1.call-update) | async-done | bytes 1843216 | tf_op jit(solution)/shard_map/all_gather | solution.py:44
  36.5 1.6 fusion.14
  38.1 1.5 convolution_add_fusion.14
  39.6 1.4 convolution_add_fusion.13
  41.0 0.4 convolution_add_fusion.12
  41.4 0.4 convolution_add_fusion.11
  41.8 0.2 copy-done.17
  42.0 0.4 convolution_add_fusion.10
  42.4 0.0 copy-done.16
  42.4 0.4 convolution_add_fusion.9
  42.8 0.1 copy-done.15
  42.9 0.4 convolution_add_fusion.8
  43.3 0.2 copy-done.20
  43.4 1.4 multiply_convert_fusion
  44.8 1.9 %copy.13 = bf16[512,320]{1,0:T(8,128)(2,1)} copy(bf16[512,320]{0,1:T(8,128)(2,1)} %get-tuple-element.22) | data formatting | bytes 655360 | tf_op jit(solution)/shard_map/convert_element_type | solution.py:58
  46.7 1.3 collective-permute-start.1
  48.0 5.9 %collective-permute-start = (bf16[1,1,16,32,320]{4,3,2,1,0:T(8,128)(2,1)}, bf16[1,1,16,32,320]{4,3,2,1,0:T(8,128)(2,1)}, u32[]{:S(2)}, u32[]{:S(2)}) collective-permute-start(bf16[1,1,16,32,320]{4,3,2,1,0:T(8,128)(2,1)} %bitcast.146), channel_id=1, source_target_pairs={{0,4},{4,8},{8,12},{12,16},{16,20},{20,24},{24,28},{1,5},{5,9},{9,... | collective-permute-start | bytes 983048 | tf_op jit(solution)/shard_map/ppermute | solution.py:16
  53.9 2.8 %fusion.9 = bf16[512,320]{0,1:T(8,128)(2,1)} fusion(f32[512,320]{0,1:T(8,128)} %fusion.21, f32[512,320]{0,1:T(8,128)} %fusion.19, bf16[512,320]{1,0:T(8,128)(2,1)} %bitcast.26, f32[512,320]{0,1:T(8,128)} %get-tuple-element.23, bf16[3,320,320]{2,1,0:T(8,128)(2,1)S(1)} %all_gather.7), kind=kOutput, calls=%fused_computation.25 | convolution fusion | flops 106659840 | bytes 2867200 | tf_op jit(solution)/shard_map/dot_general | solution.py:32
  56.7 1.9 %copy.15 = bf16[512,320]{1,0:T(8,128)(2,1)} copy(bf16[512,320]{0,1:T(8,128)(2,1)} %fusion.9) | data formatting | bytes 655360 | tf_op jit(solution)/shard_map/convert_element_type | solution.py:82
  58.6 4.4 %pad_slice_fusion.4 = (bf16[1,1,16,32,320]{4,3,2,1,0:T(8,128)(2,1)}, bf16[1,1,16,32,320]{4,3,2,1,0:T(8,128)(2,1)}, bf16[1,1,16,32,320]{4,3,2,1,0:T(8,128)(2,1)},...) fusion(bf16[1,1,16,32,320]{4,3,2,1,0:T(8,128)(2,1)} %bitcast.132), kind=kLoop, calls=%fused_computation.35 | loop fusion | bytes 2949120 | tf_op jit(solution)/shard_map/slice | solution.py:92
  63.0 1.2 fusion.15
  64.3 0.3 convolution_bitcast_fusion.1
  64.6 1.4 convolution_bitcast_fusion
  66.0 3.7 %collective-permute-done = bf16[1,1,16,32,320]{4,3,2,1,0:T(8,128)(2,1)} collective-permute-done((bf16[1,1,16,32,320]{4,3,2,1,0:T(8,128)(2,1)}, bf16[1,1,16,32,320]{4,3,2,1,0:T(8,128)(2,1)}, u32[]{:S(2)}, u32[]{:S(2)}) %collective-permute-start) | collective-permute-done | bytes 327712 | tf_op jit(solution)/shard_map/ppermute | solution.py:16
  69.6 1.3 convolution_bitcast_fusion.2
  71.0 1.2 pad_maximum_fusion
  72.3 0.0 reduce-scatter.2.cloned.1.call-update
  72.3 0.0 all-reduce.4.cloned.1.call-start
  72.3 1.4 fusion.16
  73.8 1.4 fusion.17
  75.2 0.4 fusion.18
  75.6 0.4 convolution_add_fusion.4
  76.0 0.4 convolution_add_fusion.3
  76.4 0.2 copy-done.12
  76.6 0.4 convolution_add_fusion.2
  77.0 0.1 copy-done.11
  77.0 0.4 convolution_add_fusion.1
  77.4 0.1 copy-done.8
  77.5 0.1 copy-done.19
  77.6 1.2 fusion.3
  78.9 2.3 %copy.17 = f32[512,320]{1,0:T(8,128)} copy(f32[512,320]{0,1:T(8,128)} %fusion.3) | data formatting | bytes 1310720 | tf_op jit(solution)/shard_map/add | solution.py:95
  81.1 0.4 fusion.20
  81.5 20.0 %reduce-scatter.2.cloned.1.call-done = f32[3,80,320]{2,1,0:T(8,128)} async-done(((f32[3,320,320]{2,1,0:T(8,128)}), f32[3,80,320]{2,1,0:T(8,128)}) %reduce-scatter.2.cloned.1.call-update) | async-done | bytes 307216 | tf_op jit(solution)/shard_map/reduce_scatter | solution.py:80
  101.5 0.0 all-reduce.4.cloned.1.call-update
  101.6 1.4 fusion.22
  103.0 2.3 %fusion.7 = f32[512,320]{0,1:T(8,128)} fusion(f32[512,320]{0,1:T(8,128)S(1)} %fusion.22, f32[512,320]{0,1:T(8,128)S(1)} %fusion.20, bf16[512,320]{1,0:T(8,128)(2,1)} %bitcast.19, bf16[3,320,320]{2,1,0:T(8,128)(2,1)S(1)} %all_gather.7), kind=kOutput, calls=%fused_computation.15 | convolution fusion | flops 105185280 | bytes 2539520 | tf_op jit(solution)/shard_map/dot_general | solution.py:63
  105.2 1.3 copy.14
  106.6 1.0 add.101
  107.6 69.0 %all-reduce.4.cloned.1.call-done = f32[3,80,320]{2,1,0:T(8,128)} async-done(((f32[3,80,320]{2,1,0:T(8,128)}), f32[3,80,320]{2,1,0:T(8,128)}) %all-reduce.4.cloned.1.call-update) | async-done | bytes 307216 | tf_op jit(solution)/shard_map/psum | solution.py:79
  176.5 1.7 broadcast_multiply_fusion
  (40 shorter events, 0.2 us)
Async XLA Ops:
  7.2 8.2 %copy-start.4 = (f32[1,1,16,32,320]{4,3,2,1,0:T(8,128)S(1)}, f32[1,1,16,32,320]{4,3,2,1,0:T(8,128)}, u32[]{:S(2)}) copy-start(f32[1,1,16,32,320]{4,3,2,1,0:T(8,128)} %param.5) | copy-start | bytes 1966084
  7.2 8.2 %copy-start.21 = (f32[3,80,320]{2,1,0:T(8,128)S(1)}, f32[3,80,320]{2,1,0:T(8,128)}, u32[]{:S(2)}) copy-start(f32[3,80,320]{2,1,0:T(8,128)} %param.8) | copy-start | bytes 921604
  7.2 29.3 %all-gather.2.cloned.1.call-start = ((), (), s32[]{:S(2)}) async-start(), calls=%async_computation.1 | async-start | bytes 2764800 | tf_op jit(solution)/shard_map/all_gather | solution.py:44
  7.9 93.6 %reduce-scatter.2.cloned.1.call-start = ((), (), s32[]{:S(2)}) async-start(), calls=%async_computation.2 | async-start | bytes 1843200 | tf_op jit(solution)/shard_map/reduce_scatter | solution.py:80
  9.2 21.7 %collective-permute-start.3 = (bf16[1,1,16,32,320]{4,3,2,1,0:T(8,128)(2,1)S(1)}, bf16[1,1,16,32,320]{4,3,2,1,0:T(8,128)(2,1)S(1)}, u32[]{:S(2)}, u32[]{:S(2)}) collective-permute-start(bf16[1,1,16,32,320]{4,3,2,1,0:T(8,128)(2,1)S(1)} %convert_element_type.21), channel_id=1, source_target_pairs={{0,4},{4,8},{8,12},{12,16},{16,20},{20,24},{24,28},{1,5},{5,9},{9,... | collective-permute-start | bytes 983048 | tf_op jit(solution)/shard_map/ppermute | solution.py:16
  14.1 39.9 %collective-permute-start.2 = (bf16[1,1,16,32,320]{4,3,2,1,0:T(8,128)(2,1)S(1)}, bf16[1,1,16,32,320]{4,3,2,1,0:T(8,128)(2,1)}, u32[]{:S(2)}, u32[]{:S(2)}) collective-permute-start(bf16[1,1,16,32,320]{4,3,2,1,0:T(8,128)(2,1)S(1)} %convert_element_type.21), channel_id=1, source_target_pairs={{4,0},{8,4},{12,8},{16,12},{20,16},{24,20},{28,24},{5,1},{9,5},{13... | collective-permute-start | bytes 983048 | tf_op jit(solution)/shard_map/ppermute | solution.py:18
  15.4 11.9 %copy-start.1 = (bf16[1,1,16,32,320]{4,3,2,1,0:T(8,128)(2,1)}, bf16[1,1,16,32,320]{4,3,2,1,0:T(8,128)(2,1)S(1)}, u32[]{:S(2)}) copy-start(bf16[1,1,16,32,320]{4,3,2,1,0:T(8,128)(2,1)S(1)} %convert_element_type.18) | copy-start | bytes 983044
  15.5 11.9 %copy-start.3 = (f32[1,1,16,32,320]{4,3,2,1,0:T(8,128)S(1)}, f32[1,1,16,32,320]{4,3,2,1,0:T(8,128)}, u32[]{:S(2)}) copy-start(f32[1,1,16,32,320]{4,3,2,1,0:T(8,128)} %param.9) | copy-start | bytes 1966084
  36.5 3.1 %copy-start = (bf16[9,320,320]{2,1,0:T(8,128)(2,1)S(1)}, bf16[9,320,320]{2,1,0:T(8,128)(2,1)}, u32[]{:S(2)}) copy-start(bf16[9,320,320]{2,1,0:T(8,128)(2,1)} %all-gather.2.cloned.1.call-done) | copy-start | bytes 5529604
  38.1 3.0 %copy-start.18 = (bf16[1,1,16,32,320]{4,3,2,1,0:T(8,128)(2,1)S(1)}, bf16[1,1,16,32,320]{4,3,2,1,0:T(8,128)(2,1)}, u32[]{:S(2)}) copy-start(bf16[1,1,16,32,320]{4,3,2,1,0:T(8,128)(2,1)} %get-tuple-element.17) | copy-start | bytes 983044
  39.6 1.9 %copy-start.2 = (bf16[1,1,16,32,320]{4,3,2,1,0:T(8,128)(2,1)S(1)}, bf16[1,1,16,32,320]{4,3,2,1,0:T(8,128)(2,1)}, u32[]{:S(2)}) copy-start(bf16[1,1,16,32,320]{4,3,2,1,0:T(8,128)(2,1)} %copy-done.1) | copy-start | bytes 983044
  41.0 1.0 copy-start.17
  41.4 1.0 copy-start.16
  41.8 1.1 copy-start.15
  42.4 1.0 copy-start.20
  42.4 1.0 copy-start.22
  46.7 17.9 %collective-permute-start.1 = (bf16[1,1,16,32,320]{4,3,2,1,0:T(8,128)(2,1)}, bf16[1,1,16,32,320]{4,3,2,1,0:T(8,128)(2,1)}, u32[]{:S(2)}, u32[]{:S(2)}) collective-permute-start(bf16[1,1,16,32,320]{4,3,2,1,0:T(8,128)(2,1)} %bitcast.145), channel_id=1, source_target_pairs={{4,0},{8,4},{12,8},{16,12},{20,16},{24,20},{28,24},{5,1},{9,5},{13... | collective-permute-start | bytes 983048 | tf_op jit(solution)/shard_map/ppermute | solution.py:18
  48.0 21.6 %collective-permute-start = (bf16[1,1,16,32,320]{4,3,2,1,0:T(8,128)(2,1)}, bf16[1,1,16,32,320]{4,3,2,1,0:T(8,128)(2,1)}, u32[]{:S(2)}, u32[]{:S(2)}) collective-permute-start(bf16[1,1,16,32,320]{4,3,2,1,0:T(8,128)(2,1)} %bitcast.146), channel_id=1, source_target_pairs={{0,4},{4,8},{8,12},{12,16},{16,20},{20,24},{24,28},{1,5},{5,9},{9,... | collective-permute-start | bytes 983048 | tf_op jit(solution)/shard_map/ppermute | solution.py:16
  58.6 5.6 %copy-start.6 = (bf16[512,320]{0,1:T(8,128)(2,1)S(1)}, bf16[512,320]{0,1:T(8,128)(2,1)}, u32[]{:S(2)}) copy-start(bf16[512,320]{0,1:T(8,128)(2,1)} %get-tuple-element.22) | copy-start | bytes 983044
  72.2 3.0 %copy-start.10 = (bf16[1,1,16,32,320]{4,3,2,1,0:T(8,128)(2,1)S(1)}, bf16[1,1,16,32,320]{4,3,2,1,0:T(8,128)(2,1)}, u32[]{:S(2)}) copy-start(bf16[1,1,16,32,320]{4,3,2,1,0:T(8,128)(2,1)} %get-tuple-element.12) | copy-start | bytes 983044
  72.3 104.3 %all-reduce.4.cloned.1.call-start = ((), (), s32[]{:S(2)}) async-start(), calls=%async_computation.3 | async-start | bytes 737280 | tf_op jit(solution)/shard_map/psum | solution.py:79
  72.3 3.3 %copy-start.9 = (f32[512,320]{0,1:T(8,128)S(1)}, f32[512,320]{0,1:T(8,128)}, u32[]{:S(2)}) copy-start(f32[512,320]{0,1:T(8,128)} %copy.16) | copy-start | bytes 1966084
  72.3 3.3 %copy-start.14 = (bf16[1,1,16,32,320]{4,3,2,1,0:T(8,128)(2,1)S(1)}, bf16[1,1,16,32,320]{4,3,2,1,0:T(8,128)(2,1)}, u32[]{:S(2)}) copy-start(bf16[1,1,16,32,320]{4,3,2,1,0:T(8,128)(2,1)} %get-tuple-element.13) | copy-start | bytes 983044
  73.8 2.2 %copy-start.13 = (bf16[1,1,16,32,320]{4,3,2,1,0:T(8,128)(2,1)S(1)}, bf16[1,1,16,32,320]{4,3,2,1,0:T(8,128)(2,1)}, u32[]{:S(2)}) copy-start(bf16[1,1,16,32,320]{4,3,2,1,0:T(8,128)(2,1)} %get-tuple-element.7) | copy-start | bytes 983044
  75.6 1.0 copy-start.12
  76.0 1.0 copy-start.11
  76.4 1.1 copy-start.8
  76.4 1.2 copy-start.19
  77.6 3.5 %copy-start.7 = (bf16[512,320]{0,1:T(8,128)(2,1)S(1)}, bf16[512,320]{0,1:T(8,128)(2,1)}, u32[]{:S(2)}) copy-start(bf16[512,320]{0,1:T(8,128)(2,1)} %get-tuple-element.22) | copy-start | bytes 983044
  102.9 3.7 %copy-start.5 = (f32[1,1,16,32,320]{4,3,2,1,0:T(8,128)S(1)}, f32[1,1,16,32,320]{4,3,2,1,0:T(8,128)}, u32[]{:S(2)}) copy-start(f32[1,1,16,32,320]{4,3,2,1,0:T(8,128)} %param.5) | copy-start | bytes 1966084
Sparse Core Ops, SparseCore 0:
  9.6 26.8 all-gather.1
  72.4 29.1 reduce-scatter.1
  104.9 71.5 all-reduce.3
where the time goes:
time: 186 us; the launch traced here: 185 us
  waiting for transfers between devices  99 us (53%)
  matrix products  27.1 us (15%)
  local copies, waits for them, and re-layouts  15.7 us (8%)
  between operations  14.2 us (8%)
  starting transfers between devices  13.5 us (7%)
  blocking collectives  10.1 us (5%)
  other arithmetic  5.23 us (3%)
    psum x1, waiting for transfers between devices, on_device(): summed = lax.psum(local_grad, 'tm')  69 us
    reduce_scatter x1, waiting for transfers between devices, on_device(): owned = lax.psum_scatter(summed, 'clip', scatter_dimension=1, tiled=True)  20 us
    dot_general x12, matrix products, transpose_dot(): lax.dot_general(left, right, (((1,), (1,)), ((), ())), preferred_element_...  12.3 us
    ppermute x2, starting transfers between devices, padded_2(): lax.ppermute(tail, axis, [(i, (i + 1) % count) for i in range(ends)])  10.8 us
    all_gather x1, blocking collectives, on_device(): lax.all_gather(temporal_b, 'clip', axis=1, tiled=True)  10.1 us
    dot_general x9, matrix products, on_device(): jnp.dot(window, spatial_all[3 * shift_y + shift_x], preferred_element_typ...  7.74 us
    ppermute x2, waiting for transfers between devices, padded_2(): lax.ppermute(tail, axis, [(i, (i + 1) % count) for i in range(ends)])  4.81 us
    all_gather x1, waiting for transfers between devices, on_device(): lax.all_gather(spatial_w, 'clip', axis=1, tiled=True)  4.46 us
  transfers between devices with their start and end apart: 7, of which 5 were waited for; matrix products, arithmetic and copies ran while one was open for 23% of the time, Pallas kernels for 0%

commit v1 on v0

--- a/solution.py
+++ b/solution.py
@@ -76,7 +76,9 @@
         grads.append(outer_dot(shifted_hid, cot_flat))
     local_grad = jnp.stack(grads)
     total_rows = row_count * lax.axis_size("tm") * lax.axis_size("clip")
-    summed = lax.psum(local_grad, "tm")
+    summed = local_grad
+    for hop in (1, 2, 4):
+        summed = summed + lax.ppermute(summed, "tm", [(dev, dev ^ hop) for dev in range(8)])
     owned = lax.psum_scatter(summed, "clip", scatter_dimension=1, tiled=True)
     grad_temporal = owned * (1.0 / math.sqrt(total_rows))
     grad_spatial = (grad_hidden * sigmoid_s * (1.0 + spatial * (1.0 - sigmoid_s))).astype(

time: 186 us -> 254 us (1.37)
  waiting for transfers between devices: 99 us -> 160 us
  other arithmetic: 5.23 us -> 12.3 us
  starting transfers between devices: 13.5 us -> 18.4 us
  blocking collectives: 10.1 us -> 7.38 us
    psum x1 -> x0, waiting for transfers between devices: 69 us -> none  [on_device(): summed = lax.psum(local_grad, 'tm')]
    ppermute x0 -> x3, waiting for transfers between devices: none -> 67.1 us  [on_device(): lax.ppermute(summed, 'tm', [(dev, dev ^ hop) for dev in range(8)])]
    reduce_scatter x1, waiting for transfers between devices: 20 us -> 55.2 us  [on_device(): owned = lax.psum_scatter(summed, 'clip', scatter_dimension=1, tiled=True)]
    all_gather x1, waiting for transfers between devices: 4.46 us -> 24.8 us  [on_device(): lax.all_gather(spatial_w, 'clip', axis=1, tiled=True)]
    add x0 -> x3, other arithmetic: none -> 7.45 us  [on_device(): summed + lax.ppermute(summed, 'tm', [(dev, dev ^ hop) for dev in range(8)])]
    ppermute x0 -> x3, starting transfers between devices: none -> 7.19 us  [on_device(): lax.ppermute(summed, 'tm', [(dev, dev ^ hop) for dev in range(8)])]
    ppermute x2, waiting for transfers between devices: 0.01 us -> 5.22 us  [padded_2(): lax.ppermute(head, axis, [((i + 1) % count, i) for i in range(ends)])]
    all_gather x1, blocking collectives: 10.1 us -> 7.38 us  [on_device(): lax.all_gather(temporal_b, 'clip', axis=1, tiled=True)]
  transfers between devices with their start and end apart: 7 -> 9, of which waited for: 5 -> 7; matrix products, arithmetic and copies ran while one was open for 23% -> 14% of each run, Pallas kernels for 0% -> 0%
where the time goes in v1:
time: 254 us; the launch traced here: 253 us
  waiting for transfers between devices  160 us (63%)
  matrix products  25.1 us (10%)
  starting transfers between devices  18.4 us (7%)
  local copies, waits for them, and re-layouts  15.6 us (6%)
  between operations  14.5 us (6%)
  other arithmetic  12.3 us (5%)
  blocking collectives  7.38 us (3%)
    ppermute x3, waiting for transfers between devices, on_device(): lax.ppermute(summed, 'tm', [(dev, dev ^ hop) for dev in range(8)])  67.1 us
    reduce_scatter x1, waiting for transfers between devices, on_device(): owned = lax.psum_scatter(summed, 'clip', scatter_dimension=1, tiled=True)  55.2 us
    all_gather x1, waiting for transfers between devices, on_device(): lax.all_gather(spatial_w, 'clip', axis=1, tiled=True)  24.8 us
    dot_general x12, matrix products, transpose_dot(): lax.dot_general(left, right, (((1,), (1,)), ((), ())), preferred_element_...  12.3 us
    ppermute x2, starting transfers between devices, padded_2(): lax.ppermute(tail, axis, [(i, (i + 1) % count) for i in range(ends)])  8.53 us
    add x3, other arithmetic, on_device(): summed + lax.ppermute(summed, 'tm', [(dev, dev ^ hop) for dev in range(8)])  7.45 us
    all_gather x1, blocking collectives, on_device(): lax.all_gather(temporal_b, 'clip', axis=1, tiled=True)  7.38 us
    ppermute x3, starting transfers between devices, on_device(): lax.ppermute(summed, 'tm', [(dev, dev ^ hop) for dev in range(8)])  7.19 us
  transfers between devices with their start and end apart: 9, of which 7 were waited for; matrix products, arithmetic and copies ran while one was open for 14% of the time, Pallas kernels for 0%

profile of v1, /device:TPU:0, one launch (start us, length us, event | category | flops | bytes accessed | tf_op | source)
XLA Modules:
  0.0 253.3 jit_solution(659013013654978673)
XLA Ops:
  7.2 0.7 all-gather.2.cloned.1.call-update
  7.9 1.2 convert_element_type.18
  9.1 1.6 pad_slice_fusion.8
  10.7 24.8 %all-gather.2.cloned.1.call-done = bf16[9,320,320]{2,1,0:T(8,128)(2,1)} async-done(((bf16[9,80,320]{2,1,0:T(8,128)(2,1)}), bf16[9,320,320]{2,1,0:T(8,128)(2,1)}) %all-gather.2.cloned.1.call-update) | async-done | bytes 1843216 | tf_op jit(solution)/shard_map/all_gather | solution.py:44
  35.5 1.5 fusion.14
  37.0 1.5 convolution_add_fusion.14
  38.5 0.4 convolution_add_fusion.13
  38.9 0.4 convolution_add_fusion.12
  39.3 0.4 convolution_add_fusion.11
  39.7 0.2 copy-done.18
  39.9 0.4 convolution_add_fusion.10
  40.3 0.4 convolution_add_fusion.9
  40.7 0.4 convolution_add_fusion.8
  41.1 0.2 copy-done.25
  41.3 1.3 multiply_convert_fusion
  42.6 0.9 copy.13
  43.5 1.3 collective-permute-start.1
  44.8 0.8 convert_element_type.21
  45.6 4.6 %collective-permute-start = (bf16[1,1,16,32,320]{4,3,2,1,0:T(8,128)(2,1)}, bf16[1,1,16,32,320]{4,3,2,1,0:T(8,128)(2,1)S(1)}, u32[]{:S(2)}, u32[]{:S(2)}) collective-permute-start(bf16[1,1,16,32,320]{4,3,2,1,0:T(8,128)(2,1)} %bitcast.146), channel_id=1, source_target_pairs={{0,4},{4,8},{8,12},{12,16},{16,20},{20,24},{24,28},{1,5},{5,9},{9,... | collective-permute-start | bytes 983048 | tf_op jit(solution)/shard_map/ppermute | solution.py:16
  50.2 1.4 convolution_bitcast_fusion.1
  51.6 5.2 %collective-permute-done.1 = bf16[1,1,16,32,320]{4,3,2,1,0:T(8,128)(2,1)S(1)} collective-permute-done((bf16[1,1,16,32,320]{4,3,2,1,0:T(8,128)(2,1)}, bf16[1,1,16,32,320]{4,3,2,1,0:T(8,128)(2,1)S(1)}, u32[]{:S(2)}, u32[]{:S(2)}) %collective-permute-start.1) | collective-permute-done | bytes 327712 | tf_op jit(solution)/shard_map/ppermute | solution.py:18
  56.8 1.5 convolution_bitcast_fusion
  58.4 6.9 %collective-permute-done = bf16[1,1,16,32,320]{4,3,2,1,0:T(8,128)(2,1)S(1)} collective-permute-done((bf16[1,1,16,32,320]{4,3,2,1,0:T(8,128)(2,1)}, bf16[1,1,16,32,320]{4,3,2,1,0:T(8,128)(2,1)S(1)}, u32[]{:S(2)}, u32[]{:S(2)}) %collective-permute-start) | collective-permute-done | bytes 327712 | tf_op jit(solution)/shard_map/ppermute | solution.py:16
  65.3 1.5 convolution_bitcast_fusion.2
  66.9 2.4 collective-permute-start.4
  69.4 32.5 %collective-permute-done.4 = f32[3,320,320]{2,1,0:T(8,128)S(1)} collective-permute-done((f32[3,320,320]{2,1,0:T(8,128)S(1)}, f32[3,320,320]{2,1,0:T(8,128)S(1)}, u32[]{:S(2)}, u32[]{:S(2)}) %collective-permute-start.4) | collective-permute-done | bytes 1228832 | tf_op jit(solution)/shard_map/ppermute | solution.py:81
  101.8 1.5 fusion.23
  103.4 1.9 collective-permute-start.5
  105.3 4.0 %collective-permute-start.3 = (bf16[1,1,16,32,320]{4,3,2,1,0:T(8,128)(2,1)}, bf16[1,1,16,32,320]{4,3,2,1,0:T(8,128)(2,1)}, u32[]{:S(2)}, u32[]{:S(2)}) collective-permute-start(bf16[1,1,16,32,320]{4,3,2,1,0:T(8,128)(2,1)} %convert_element_type.21), channel_id=1, source_target_pairs={{0,4},{4,8},{8,12},{12,16},{16,20},{20,24},{24,28},{1,5},{5,9},{9,... | collective-permute-start | bytes 983048 | tf_op jit(solution)/shard_map/ppermute | solution.py:16
  109.2 1.3 collective-permute-start.2
  110.6 7.4 %all_gather.7 = bf16[3,320,320]{2,1,0:T(8,128)(2,1)S(1)} all-gather(bf16[3,80,320]{2,1,0:T(8,128)(2,1)S(1)} %convert_element_type.20), channel_id=1, replica_groups=mesh['tm'=8,'clip'=4] {'clip'}, dimensions={1}, use_global_device_ids=true | all-gather | bytes 768000 | tf_op jit(solution)/shard_map/all_gather | solution.py:45
  118.0 2.3 copy.16
  120.2 1.5 fusion.19
  121.7 1.4 fusion.21
  123.1 15.7 %collective-permute-done.5 = f32[3,320,320]{2,1,0:T(8,128)} collective-permute-done((f32[3,320,320]{2,1,0:T(8,128)}, f32[3,320,320]{2,1,0:T(8,128)}, u32[]{:S(2)}, u32[]{:S(2)}) %collective-permute-start.5) | collective-permute-done | bytes 1228832 | tf_op jit(solution)/shard_map/ppermute | solution.py:81
  138.8 2.8 %fusion.50 = f32[3,320,320]{2,1,0:T(8,128)} fusion(f32[3,320,320]{2,1,0:T(8,128)} %collective-permute-done.5, f32[3,320,320]{2,1,0:T(8,128)S(1)} %copy-done.2, f32[1,320,320]{2,1,0:T(8,128)S(1)} %copy-done.4, f32[1,320,320]{2,1,0:T(8,128)S(1)} %convolution_bitcast_fusion.1, f32[1,320,320]{2,1,0:T(8,128)S(1)} %copy-done.6), kind=kLoop, calls=%fused_computation.74 | loop fusion | flops 1228800 | bytes 4915200 | tf_op jit(solution)/shard_map/add | solution.py:81
  141.7 2.8 %collective-permute-start.6 = (f32[3,320,320]{2,1,0:T(8,128)}, f32[3,320,320]{2,1,0:T(8,128)}, u32[]{:S(2)}, u32[]{:S(2)}) collective-permute-start(f32[3,320,320]{2,1,0:T(8,128)} %fusion.50), channel_id=1, source_target_pairs={{0,16},{4,20},{8,24},{12,28},{16,0},{20,4},{24,8},{28,12},{1,17},{... | collective-permute-start | bytes 3686408 | tf_op jit(solution)/shard_map/ppermute | solution.py:81
  144.5 1.5 fusion.9
  146.0 0.9 copy.15
  146.9 4.8 %pad_slice_fusion.4 = (bf16[1,1,16,32,320]{4,3,2,1,0:T(8,128)(2,1)}, bf16[1,1,16,32,320]{4,3,2,1,0:T(8,128)(2,1)}, bf16[1,1,16,32,320]{4,3,2,1,0:T(8,128)(2,1)},...) fusion(bf16[1,1,16,32,320]{4,3,2,1,0:T(8,128)(2,1)} %bitcast.130), kind=kLoop, calls=%fused_computation.35 | loop fusion | bytes 2949120 | tf_op jit(solution)/shard_map/slice | solution.py:94
  151.7 1.2 fusion.18
  152.9 1.2 fusion.17
  154.1 1.2 fusion.16
  155.3 18.9 %collective-permute-done.6 = f32[3,320,320]{2,1,0:T(8,128)} collective-permute-done((f32[3,320,320]{2,1,0:T(8,128)}, f32[3,320,320]{2,1,0:T(8,128)}, u32[]{:S(2)}, u32[]{:S(2)}) %collective-permute-start.6) | collective-permute-done | bytes 1228832 | tf_op jit(solution)/shard_map/ppermute | solution.py:81
  174.2 3.1 %add.123 = f32[3,320,320]{2,1,0:T(8,128)} add(f32[3,320,320]{2,1,0:T(8,128)} %fusion.50, f32[3,320,320]{2,1,0:T(8,128)} %collective-permute-done.6) | non-fusion elementwise | flops 307200 | bytes 3686400 | tf_op jit(solution)/shard_map/add | solution.py:81
  177.4 0.4 fusion.15
  177.8 1.6 convolution_add_fusion.4
  179.4 0.4 convolution_add_fusion.3
  179.8 0.4 convolution_add_fusion.2
  180.2 0.2 copy-done.14
  180.4 0.4 convolution_add_fusion.1
  180.8 0.1 copy-done.11
  180.9 0.2 copy-done.12
  181.1 0.2 copy-done.13
  181.4 1.2 fusion.3
  182.6 2.3 copy.17
  184.9 0.4 fusion.20
  185.3 0.4 fusion.22
  185.7 0.2 copy-done.24
  185.9 1.2 fusion.7
  187.1 1.3 copy.14
  188.5 1.0 add.108
  189.5 55.2 %reduce-scatter.2.cloned.1.call-done = f32[3,80,320]{2,1,0:T(8,128)} async-done(((f32[3,320,320]{2,1,0:T(8,128)}), f32[3,80,320]{2,1,0:T(8,128)}) %reduce-scatter.2.cloned.1.call-update) | async-done | bytes 307216 | tf_op jit(solution)/shard_map/reduce_scatter | solution.py:82
  244.7 1.7 broadcast_multiply_fusion
  (62 shorter events, 0.5 us)
Async XLA Ops:
  7.2 28.3 %all-gather.2.cloned.1.call-start = ((), (), s32[]{:S(2)}) async-start(), calls=%async_computation.1 | async-start | bytes 2764800 | tf_op jit(solution)/shard_map/all_gather | solution.py:44
  7.9 236.8 %reduce-scatter.2.cloned.1.call-start = ((), (), s32[]{:S(2)}) async-start(), calls=%async_computation.2 | async-start | bytes 1843200 | tf_op jit(solution)/shard_map/reduce_scatter | solution.py:82
  35.5 3.0 %copy-start = (bf16[9,320,320]{2,1,0:T(8,128)(2,1)S(1)}, bf16[9,320,320]{2,1,0:T(8,128)(2,1)}, u32[]{:S(2)}) copy-start(bf16[9,320,320]{2,1,0:T(8,128)(2,1)} %all-gather.2.cloned.1.call-done) | copy-start | bytes 5529604
  35.5 3.0 %copy-start.20 = (bf16[1,1,16,32,320]{4,3,2,1,0:T(8,128)(2,1)S(1)}, bf16[1,1,16,32,320]{4,3,2,1,0:T(8,128)(2,1)}, u32[]{:S(2)}) copy-start(bf16[1,1,16,32,320]{4,3,2,1,0:T(8,128)(2,1)} %get-tuple-element.16) | copy-start | bytes 983044
  37.0 1.9 copy-start.19
  38.9 1.0 copy-start.18
  39.3 1.0 copy-start.17
  40.3 1.0 copy-start.25
  40.3 1.0 copy-start.29
  41.3 3.5 %copy-start.7 = (f32[1,1,16,32,320]{4,3,2,1,0:T(8,128)S(1)}, f32[1,1,16,32,320]{4,3,2,1,0:T(8,128)}, u32[]{:S(2)}) copy-start(f32[1,1,16,32,320]{4,3,2,1,0:T(8,128)} %param.9) | copy-start | bytes 1966084
  42.6 7.6 %copy-start.9 = (bf16[512,320]{0,1:T(8,128)(2,1)}, bf16[512,320]{0,1:T(8,128)(2,1)S(1)}, u32[]{:S(2)}) copy-start(bf16[512,320]{0,1:T(8,128)(2,1)S(1)} %get-tuple-element.22) | copy-start | bytes 983044
  43.5 13.3 %collective-permute-start.1 = (bf16[1,1,16,32,320]{4,3,2,1,0:T(8,128)(2,1)}, bf16[1,1,16,32,320]{4,3,2,1,0:T(8,128)(2,1)S(1)}, u32[]{:S(2)}, u32[]{:S(2)}) collective-permute-start(bf16[1,1,16,32,320]{4,3,2,1,0:T(8,128)(2,1)} %bitcast.145), channel_id=1, source_target_pairs={{4,0},{8,4},{12,8},{16,12},{20,16},{24,20},{28,24},{5,1},{9,5},{13... | collective-permute-start | bytes 983048 | tf_op jit(solution)/shard_map/ppermute | solution.py:18
  45.6 19.6 %collective-permute-start = (bf16[1,1,16,32,320]{4,3,2,1,0:T(8,128)(2,1)}, bf16[1,1,16,32,320]{4,3,2,1,0:T(8,128)(2,1)S(1)}, u32[]{:S(2)}, u32[]{:S(2)}) collective-permute-start(bf16[1,1,16,32,320]{4,3,2,1,0:T(8,128)(2,1)} %bitcast.146), channel_id=1, source_target_pairs={{0,4},{4,8},{8,12},{12,16},{16,20},{20,24},{24,28},{1,5},{5,9},{9,... | collective-permute-start | bytes 983048 | tf_op jit(solution)/shard_map/ppermute | solution.py:16
  56.8 8.4 %copy-start.26 = (bf16[1,1,16,32,320]{4,3,2,1,0:T(8,128)(2,1)}, bf16[1,1,16,32,320]{4,3,2,1,0:T(8,128)(2,1)S(1)}, u32[]{:S(2)}) copy-start(bf16[1,1,16,32,320]{4,3,2,1,0:T(8,128)(2,1)S(1)} %collective-permute-done.1) | copy-start | bytes 983044
  58.4 43.5 %copy-start.3 = (f32[1,320,320]{2,1,0:T(8,128)}, f32[1,320,320]{2,1,0:T(8,128)S(1)}, u32[]{:S(2)}) copy-start(f32[1,320,320]{2,1,0:T(8,128)S(1)} %convolution_bitcast_fusion) | copy-start | bytes 1228804
  65.3 1.6 copy-start.23
  66.8 36.6 %copy-start.5 = (f32[1,320,320]{2,1,0:T(8,128)}, f32[1,320,320]{2,1,0:T(8,128)S(1)}, u32[]{:S(2)}) copy-start(f32[1,320,320]{2,1,0:T(8,128)S(1)} %convolution_bitcast_fusion.2) | copy-start | bytes 1228804
  66.9 43.6 %copy-start.28 = (f32[3,80,320]{2,1,0:T(8,128)S(1)}, f32[3,80,320]{2,1,0:T(8,128)}, u32[]{:S(2)}) copy-start(f32[3,80,320]{2,1,0:T(8,128)} %param.8) | copy-start | bytes 921604
  66.9 34.9 %collective-permute-start.4 = (f32[3,320,320]{2,1,0:T(8,128)S(1)}, f32[3,320,320]{2,1,0:T(8,128)S(1)}, u32[]{:S(2)}, u32[]{:S(2)}) collective-permute-start(f32[3,320,320]{2,1,0:T(8,128)S(1)} %pad_maximum_fusion), channel_id=1, source_target_pairs={{0,4},{4,0},{8,12},{12,8},{16,20},{20,16},{24,28},{28,24},{1,5},{5... | collective-permute-start | bytes 3686408 | tf_op jit(solution)/shard_map/ppermute | solution.py:81
  101.8 8.7 %copy-start.1 = (f32[3,320,320]{2,1,0:T(8,128)}, f32[3,320,320]{2,1,0:T(8,128)S(1)}, u32[]{:S(2)}) copy-start(f32[3,320,320]{2,1,0:T(8,128)S(1)} %collective-permute-done.4) | copy-start | bytes 3686404
  103.4 35.5 %collective-permute-start.5 = (f32[3,320,320]{2,1,0:T(8,128)}, f32[3,320,320]{2,1,0:T(8,128)}, u32[]{:S(2)}, u32[]{:S(2)}) collective-permute-start(f32[3,320,320]{2,1,0:T(8,128)} %fusion.23), channel_id=1, source_target_pairs={{0,8},{4,12},{8,0},{12,4},{16,24},{20,28},{24,16},{28,20},{1,9},{5... | collective-permute-start | bytes 3686408 | tf_op jit(solution)/shard_map/ppermute | solution.py:81
  105.3 16.5 %collective-permute-start.3 = (bf16[1,1,16,32,320]{4,3,2,1,0:T(8,128)(2,1)}, bf16[1,1,16,32,320]{4,3,2,1,0:T(8,128)(2,1)}, u32[]{:S(2)}, u32[]{:S(2)}) collective-permute-start(bf16[1,1,16,32,320]{4,3,2,1,0:T(8,128)(2,1)} %convert_element_type.21), channel_id=1, source_target_pairs={{0,4},{4,8},{8,12},{12,16},{16,20},{20,24},{24,28},{1,5},{5,9},{9,... | collective-permute-start | bytes 983048 | tf_op jit(solution)/shard_map/ppermute | solution.py:16
  109.2 35.3 %collective-permute-start.2 = (bf16[1,1,16,32,320]{4,3,2,1,0:T(8,128)(2,1)}, bf16[1,1,16,32,320]{4,3,2,1,0:T(8,128)(2,1)}, u32[]{:S(2)}, u32[]{:S(2)}) collective-permute-start(bf16[1,1,16,32,320]{4,3,2,1,0:T(8,128)(2,1)} %convert_element_type.21), channel_id=1, source_target_pairs={{4,0},{8,4},{12,8},{16,12},{20,16},{24,20},{28,24},{5,1},{9,5},{13... | collective-permute-start | bytes 983048 | tf_op jit(solution)/shard_map/ppermute | solution.py:18
  120.2 18.6 %copy-start.2 = (f32[3,320,320]{2,1,0:T(8,128)S(1)}, f32[3,320,320]{2,1,0:T(8,128)}, u32[]{:S(2)}) copy-start(f32[3,320,320]{2,1,0:T(8,128)} %copy-done.1) | copy-start | bytes 3686404
  120.2 18.6 %copy-start.4 = (f32[1,320,320]{2,1,0:T(8,128)S(1)}, f32[1,320,320]{2,1,0:T(8,128)}, u32[]{:S(2)}) copy-start(f32[1,320,320]{2,1,0:T(8,128)} %copy-done.3) | copy-start | bytes 1228804
  120.2 18.6 %copy-start.6 = (f32[1,320,320]{2,1,0:T(8,128)S(1)}, f32[1,320,320]{2,1,0:T(8,128)}, u32[]{:S(2)}) copy-start(f32[1,320,320]{2,1,0:T(8,128)} %copy-done.5) | copy-start | bytes 1228804
  123.1 21.4 %copy-start.30 = (f32[512,320]{0,1:T(8,128)S(1)}, f32[512,320]{0,1:T(8,128)}, u32[]{:S(2)}) copy-start(f32[512,320]{0,1:T(8,128)} %get-tuple-element.23) | copy-start | bytes 1966084
  141.7 32.6 %collective-permute-start.6 = (f32[3,320,320]{2,1,0:T(8,128)}, f32[3,320,320]{2,1,0:T(8,128)}, u32[]{:S(2)}, u32[]{:S(2)}) collective-permute-start(f32[3,320,320]{2,1,0:T(8,128)} %fusion.50), channel_id=1, source_target_pairs={{0,16},{4,20},{8,24},{12,28},{16,0},{20,4},{24,8},{28,12},{1,17},{... | collective-permute-start | bytes 3686408 | tf_op jit(solution)/shard_map/ppermute | solution.py:81
  146.0 0.9 copy-start.21
  177.4 2.0 copy-start.16
  177.8 2.1 copy-start.15
  179.4 1.0 copy-start.14
  179.8 1.1 copy-start.11
  179.8 1.3 copy-start.12
  179.8 1.5 copy-start.13
  179.8 1.6 copy-start.22
  181.4 3.5 %copy-start.10 = (bf16[512,320]{0,1:T(8,128)(2,1)S(1)}, bf16[512,320]{0,1:T(8,128)(2,1)}, u32[]{:S(2)}) copy-start(bf16[512,320]{0,1:T(8,128)(2,1)} %copy-done.9) | copy-start | bytes 983044
  182.6 2.7 %copy-start.27 = (bf16[1,1,16,32,320]{4,3,2,1,0:T(8,128)(2,1)S(1)}, bf16[1,1,16,32,320]{4,3,2,1,0:T(8,128)(2,1)}, u32[]{:S(2)}) copy-start(bf16[1,1,16,32,320]{4,3,2,1,0:T(8,128)(2,1)} %copy-done.26) | copy-start | bytes 983044
  184.9 1.0 copy-start.24
  185.7 2.8 %copy-start.8 = (f32[1,1,16,32,320]{4,3,2,1,0:T(8,128)S(1)}, f32[1,1,16,32,320]{4,3,2,1,0:T(8,128)}, u32[]{:S(2)}) copy-start(f32[1,1,16,32,320]{4,3,2,1,0:T(8,128)} %param.5) | copy-start | bytes 1966084
Sparse Core Ops, SparseCore 0:
  9.5 25.9 all-gather.1
  177.5 67.1 reduce-scatter.1
